TPU v7x, 32 devices: a whole 2x2x4 slice. The times are simulated.
32 devices in a mesh: strip: 8 (over z, x), period: 4 (over y, core).
Axes of the slice: x: 2, y: 2, z: 4, core: 2. Of those that a mesh axis runs over, the one named last changes fastest.
Arguments:
- u_start: float32 [8, 16, 64, 128], P('strip', 'period'), may hold values from 0 to 0.02
- dual_prec: float32 [5, 8, 16, 64, 128], P(None, 'strip', 'period'), may hold values from 0 to 0.5
- dual_bound: float32 [8, 16, 64, 128], P('strip', 'period'), may hold values from 0 to 0.5
- dual_cap: float32 [16], P('period'), may hold values from 0 to 2
- capacity: float32 [16], P('period'), may hold values from 0.005 to 0.03
- block_value: float32 [8, 64, 128], P('strip'), may hold values from -6 to 6
- ton_class: int32 [8, 64, 128], P('strip'), may hold values from 0 to 7
- density: float32 [8], replicated, may hold values from 1 to 3
- slope_code: int32 [8, 128], P('strip'), may hold values from 0 to 15
- omega_start: float32 [1], replicated, may hold values from 0.5 to 2
Outputs:
- mined_share: float32 [8, 16, 64, 128], P('strip', 'period')
- arc_prices: float32 [5, 8, 16, 64, 128], P(None, 'strip', 'period')
- bound_prices: float32 [8, 16, 64, 128], P('strip', 'period')
- capacity_prices: float32 [16], P('period')
- primal_weight: float32 [1], replicated
All inputs are finite; a program needn't handle non-finite values.
Results may differ from a plain program's by a relative error of at most 0.0001.
Values sent between devices are 32-bit elements; how exact they have to be, the bound alone decides.
A program may use at most 64 MiB of HBM per device.

v0:
```python
import math

import jax
import jax.numpy as jnp
from jax import lax
from jax.sharding import PartitionSpec as P

OUTER = 2
INNER = 3


ARC_OFFSETS = ((0, 0), (1, 0), (-1, 0), (0, 1), (0, -1))
RATE = math.log(1.1) / 12.0
EPS = 1e-06
SLOPE = 11.0


def from_behind(value, axis, by):
    devices = lax.axis_size(axis)
    pairs = [(i, i + by) for i in range(devices) if 0 <= i + by < devices]
    return lax.ppermute(value, axis, pairs)


def carried_in(value, axis, combine, identity, reverse):
    devices, index = (lax.axis_size(axis), lax.axis_index(axis))
    everything = lax.all_gather(value, axis)
    start = jnp.broadcast_to(jnp.asarray(identity, value.dtype), value.shape)

    def lap(k, before):
        at = devices - 1 - k if reverse else k
        reached = at > index if reverse else at < index
        new = combine(before, everything[at])
        return jnp.where(reached, new, before)

    return lax.fori_loop(0, devices, lap, start)


def padded_2(value, sides, width):
    for axis, dim in sides:
        devices, length = (lax.axis_size(axis), value.shape[dim])
        up = [(i, (i + 1) % devices) for i in range(devices - 1)]
        down = [(j, i) for i, j in up]
        last = lax.slice_in_dim(value, length - width, length, axis=dim)
        first = lax.slice_in_dim(value, 0, width, axis=dim)
        before = lax.ppermute(last, axis, up)
        after = lax.ppermute(first, axis, down)
        value = jnp.concatenate([before, value, after], axis=dim)
    return value


def arc_masks(code_rows, first_row, total_rows, depth_cells, across):
    row_ids = (first_row + jnp.arange(code_rows.shape[0]))[:, None, None]
    depth_ids = jnp.arange(depth_cells)[None, :, None]
    col_ids = jnp.arange(across)[None, None, :]
    pattern = code_rows[:, None, :]
    mask_list = []
    for arc_index, (step_x, step_y) in enumerate(ARC_OFFSETS):
        inside = (
            (row_ids >= 0)
            & (row_ids < total_rows)
            & (row_ids + step_x >= 0)
            & (row_ids + step_x < total_rows)
        )
        inside = inside & (col_ids + step_y >= 0) & (col_ids + step_y < across) & (depth_ids >= 1)
        if arc_index > 0:
            inside = inside & (pattern // 2 ** (arc_index - 1) % 2 == 1)
        mask_list.append(inside.astype(jnp.float32))
    return jnp.stack(mask_list)


def tonnage(ton_class, density):
    class_ids = jnp.arange(density.shape[0])
    class_table = (1.0 + class_ids.astype(jnp.float32)) * density
    onehot = (class_ids[:, None, None, None] == ton_class[None]).astype(jnp.float32)
    return jnp.einsum("k,kxzy->xzy", class_table, onehot, precision=lax.Precision.HIGHEST)


def upper_cell(values_in, step_y):
    depth_cells = values_in.shape[2]
    across = values_in.shape[3]
    padded = jnp.pad(values_in, ((0, 0), (0, 0), (1, 0), (1, 1)))
    return padded[:, :, 0:depth_cells, 1 + step_y : 1 + step_y + across]


def lower_cell(values_in, step_y):
    depth_cells = values_in.shape[2]
    across = values_in.shape[3]
    padded = jnp.pad(values_in, ((0, 0), (0, 0), (0, 1), (1, 1)))
    return padded[:, :, 1 : depth_cells + 1, 1 - step_y : 1 - step_y + across]


def adjoint(arc_duals, from_left, from_right, bound_duals):
    result = jnp.sum(arc_duals, axis=0) + bound_duals
    for arc_index, (step_x, step_y) in enumerate(ARC_OFFSETS):
        source = arc_duals[arc_index]
        if step_x == 1:
            source = jnp.concatenate([from_left, source[:-1]], axis=0)
        elif step_x == -1:
            source = jnp.concatenate([source[1:], from_right], axis=0)
        result = result - lower_cell(source, step_y)
    return result


def send_rims(arc_duals):
    from_left = from_behind(arc_duals[1, -1:], "strip", 1)
    from_right = from_behind(arc_duals[2, :1], "strip", -1)
    return (from_left, from_right)


def capacity_sum(row_local):
    return lax.psum(row_local, "strip")


def add_pair(earlier, later):
    return earlier + later


def per_device(
    u_start,
    dual_prec,
    dual_bound,
    dual_cap,
    capacity,
    block_value,
    ton_class,
    density,
    slope_code,
    omega_start,
):
    rows_here = u_start.shape[0]
    periods_here = u_start.shape[1]
    depth_cells = u_start.shape[2]
    across = u_start.shape[3]
    total_rows = lax.axis_size("strip") * rows_here
    total_periods = lax.axis_size("period") * periods_here
    blocks_all = float(total_rows * depth_cells * across)
    root_blocks = math.sqrt(blocks_all)
    zero_plane = jnp.zeros((rows_here, depth_cells, across), jnp.float32)
    arc_active = arc_masks(
        slope_code, lax.axis_index("strip") * rows_here, total_rows, depth_cells, across
    )[:, :, None]
    tonnage_grid = tonnage(ton_class, density)
    tons_col = tonnage_grid[:, None]
    tons_all = lax.psum(jnp.sum(tonnage_grid), "strip")
    period_ids = (lax.axis_index("period") * periods_here + jnp.arange(periods_here)).astype(
        jnp.float32
    )[None, :, None, None]
    profit = block_value[:, None] * jnp.exp(-RATE * period_ids)
    primal = u_start
    arc_duals = dual_prec * arc_active
    bound_duals = dual_bound
    cap_duals = dual_cap
    weight = omega_start[0]
    for restart in range(OUTER):
        primal_first, duals_first, bound_first, cap_first = (
            primal,
            arc_duals,
            bound_duals,
            cap_duals,
        )
        primal_sum = jnp.zeros_like(primal)
        duals_sum = jnp.zeros_like(arc_duals)
        bound_sum = jnp.zeros_like(bound_duals)
        cap_sum = jnp.zeros_like(cap_duals)
        move_primal = jnp.float32(0.0)
        move_dual = jnp.float32(0.0)
        for sweep_index in range(INNER):
            from_left, from_right = send_rims(arc_duals)
            gradient_x = adjoint(arc_duals, from_left, from_right, bound_duals)
            local_tail = jnp.flip(jnp.cumsum(jnp.flip(gradient_x, 1), axis=1), 1)
            later_sum = carried_in(local_tail[:, 0], "period", add_pair, zero_plane, True)
            gradient_u = (
                local_tail
                + later_sum[:, None]
                + tons_col * cap_duals[None, :, None, None] / root_blocks
            )
            step_primal = 1.0 / (
                weight * (SLOPE * (total_periods - period_ids) + tons_col / root_blocks)
            )
            primal_new = jnp.maximum(primal - step_primal * (gradient_u - profit), 0.0)
            extrapolated = 2.0 * primal_new - primal
            local_head = jnp.cumsum(extrapolated, axis=1)
            earlier_sum = carried_in(local_head[:, -1], "period", add_pair, zero_plane, False)
            cumulative = local_head + earlier_sum[:, None]
            padded = padded_2(cumulative, (("strip", 0),), 1)
            step_prec = weight / (2.0 * (period_ids + 1.0))
            step_bound = weight / (period_ids + 1.0)
            new_list = []
            for arc_index, (step_x, step_y) in enumerate(ARC_OFFSETS):
                ahead_cells = upper_cell(padded[1 + step_x : 1 + step_x + rows_here], step_y)
                new_list.append(
                    jnp.maximum(arc_duals[arc_index] + step_prec * (cumulative - ahead_cells), 0.0)
                    * arc_active[arc_index]
                )
            duals_new = jnp.stack(new_list)
            bound_new = jnp.maximum(bound_duals + step_bound * (cumulative - 1.0), 0.0)
            primal_sum = primal_sum + primal_new
            duals_sum = duals_sum + duals_new
            bound_sum = bound_sum + bound_new
            row_local = jnp.einsum(
                "xzy,xtzy->t", tonnage_grid, extrapolated, precision=lax.Precision.HIGHEST
            )
            if sweep_index == INNER - 1:
                primal_mean = primal_sum / INNER
                duals_mean = duals_sum / INNER
                bound_mean = bound_sum / INNER
                move_primal = jnp.sum((primal_mean - primal_first) ** 2)
                move_dual = jnp.sum((duals_mean - duals_first) ** 2) + jnp.sum(
                    (bound_mean - bound_first) ** 2
                )
                row_total, move_primal, move_dual = lax.psum(
                    (row_local, move_primal, move_dual), "strip"
                )
            else:
                row_total = capacity_sum(row_local)
            cap_new = jnp.maximum(
                cap_duals + weight * (row_total - blocks_all * capacity) / tons_all, 0.0
            )
            cap_sum = cap_sum + cap_new
            primal, arc_duals, bound_duals, cap_duals = (primal_new, duals_new, bound_new, cap_new)
        cap_mean = cap_sum / INNER
        move_cap = jnp.sum((cap_mean - cap_first) ** 2)
        primal_mean = primal_sum / INNER
        duals_mean = duals_sum / INNER
        bound_mean = bound_sum / INNER
        primal_move, dual_move = lax.psum((move_primal, move_dual + move_cap), "period")
        weight = jnp.sqrt(weight * jnp.sqrt((dual_move + EPS) / (primal_move + EPS)))
        primal = primal_mean
        arc_duals = duals_mean
        bound_duals = bound_mean
        cap_duals = cap_mean
    return (primal, arc_duals, bound_duals, cap_duals, jnp.reshape(weight, (1,)))


def solution(mesh):
    in_specs = (
        P("strip", "period", None, None),
        P(None, "strip", "period", None, None),
        P("strip", "period", None, None),
        P("period"),
        P("period"),
        P("strip", None, None),
        P("strip", None, None),
        P(),
        P("strip", None),
        P(),
    )
    out_specs = (
        P("strip", "period", None, None),
        P(None, "strip", "period", None, None),
        P("strip", "period", None, None),
        P("period"),
        P(),
    )
    return jax.shard_map(
        per_device, mesh=mesh, in_specs=in_specs, out_specs=out_specs, check_vma=False
    )
```

profile of v0, /device:TPU:0, one launch (start us, length us, event | category | flops | bytes accessed | tf_op | source)
XLA Modules:
  0.0 341.3 jit_solution(55738241060325181)
XLA Ops:
  3.1 4.9 %collective-permute-start = (f32[1,4,64,128]{3,2,1,0:T(8,128)S(1)}, f32[1,4,64,128]{3,2,1,0:T(8,128)S(1)}, u32[]{:S(2)}, u32[]{:S(2)}) collective-permute-start(f32[1,4,64,128]{3,2,1,0:T(8,128)S(1)} %get-tuple-element.1518), channel_id=1, source_target_pairs={{0,4},{4,8},{8,12},{12,16},{16,20},{20,24},{24,28},{1,5},{5,9},{9,... | collective-permute-start | bytes 393224 | tf_op jit(solution)/shard_map/ppermute | solution.py:21
  15.2 5.4 %all_gather.36 = f32[4,1,64,128]{3,2,1,0:T(8,128)S(1)} all-gather(f32[1,1,64,128]{3,2,1,0:T(8,128)S(1)} %slice.384), channel_id=1, replica_groups=mesh['strip'=8,'period'=4] {'period'}, dimensions={0}, use_global_device_ids=true | all-gather | bytes 163840 | tf_op jit(solution)/shard_map/all_gather | solution.py:26
  21.7 5.4 %all_gather.37 = f32[4,1,64,128]{3,2,1,0:T(8,128)S(1)} all-gather(f32[1,1,64,128]{3,2,1,0:T(8,128)S(1)} %slice.385), channel_id=1, replica_groups=mesh['strip'=8,'period'=4] {'period'}, dimensions={0}, use_global_device_ids=true | all-gather | bytes 163840 | tf_op jit(solution)/shard_map/all_gather | solution.py:26
  28.5 5.0 %collective-permute-start.3 = (f32[1,4,64,128]{3,2,1,0:T(8,128)S(1)}, f32[1,4,64,128]{3,2,1,0:T(8,128)S(1)}, u32[]{:S(2)}, u32[]{:S(2)}) collective-permute-start(f32[1,4,64,128]{3,2,1,0:T(8,128)S(1)} %broadcast_add_fusion.5), channel_id=1, source_target_pairs={{0,4},{4,8},{8,12},{12,16},{16,20},{20,24},{24,28},{1,5},{5,9},{9,... | collective-permute-start | bytes 393224 | tf_op jit(solution)/shard_map/ppermute | solution.py:45
  34.3 20.9 %all-reduce.50 = (f32[4]{0:T(128)S(1)}, f32[]{:T(128)}) all-reduce(f32[4]{0:T(128)S(1)} %convolution_bitcast_fusion.5, f32[]{:T(128)} %get-tuple-element.1520), channel_id=1, replica_groups=mesh['strip'=8,'period'=4] {'strip'}, use_global_device_ids=true, to_apply=%region_10.11 | all-reduce | flops 5 | bytes 40 | tf_op jit(solution)/shard_map/psum | solution.py:111
  58.1 4.6 %collective-permute-start.4 = (f32[1,4,64,128]{3,2,1,0:T(8,128)S(1)}, f32[1,4,64,128]{3,2,1,0:T(8,128)S(1)}, u32[]{:S(2)}, u32[]{:S(2)}) collective-permute-start(f32[1,4,64,128]{3,2,1,0:T(8,128)S(1)} %get-tuple-element.1501), channel_id=1, source_target_pairs={{0,4},{4,8},{8,12},{12,16},{16,20},{20,24},{24,28},{1,5},{5,9},{9,... | collective-permute-start | bytes 393224 | tf_op jit(solution)/shard_map/ppermute | solution.py:21
  65.4 5.4 %all_gather.38 = f32[4,1,64,128]{3,2,1,0:T(8,128)S(1)} all-gather(f32[1,1,64,128]{3,2,1,0:T(8,128)S(1)} %slice.386), channel_id=1, replica_groups=mesh['strip'=8,'period'=4] {'period'}, dimensions={0}, use_global_device_ids=true | all-gather | bytes 163840 | tf_op jit(solution)/shard_map/all_gather | solution.py:26
  71.2 5.4 %all_gather.39 = f32[4,1,64,128]{3,2,1,0:T(8,128)S(1)} all-gather(f32[1,1,64,128]{3,2,1,0:T(8,128)S(1)} %slice.387), channel_id=1, replica_groups=mesh['strip'=8,'period'=4] {'period'}, dimensions={0}, use_global_device_ids=true | all-gather | bytes 163840 | tf_op jit(solution)/shard_map/all_gather | solution.py:26
  79.5 5.0 %collective-permute-start.7 = (f32[1,4,64,128]{3,2,1,0:T(8,128)S(1)}, f32[1,4,64,128]{3,2,1,0:T(8,128)S(1)}, u32[]{:S(2)}, u32[]{:S(2)}) collective-permute-start(f32[1,4,64,128]{3,2,1,0:T(8,128)S(1)} %broadcast_add_fusion.4), channel_id=1, source_target_pairs={{0,4},{4,8},{8,12},{12,16},{16,20},{20,24},{24,28},{1,5},{5,9},{9,... | collective-permute-start | bytes 393224 | tf_op jit(solution)/shard_map/ppermute | solution.py:45
  84.5 20.0 %psum.107 = f32[4]{0:T(128)S(1)} all-reduce(f32[4]{0:T(128)S(1)} %convolution_bitcast_fusion.4), channel_id=1, replica_groups=mesh['strip'=8,'period'=4] {'strip'}, use_global_device_ids=true, to_apply=%region_19.20 | all-reduce | flops 4 | bytes 32 | tf_op jit(solution)/shard_map/psum | solution.py:111
  108.7 4.6 %collective-permute-start.8 = (f32[1,4,64,128]{3,2,1,0:T(8,128)S(1)}, f32[1,4,64,128]{3,2,1,0:T(8,128)S(1)}, u32[]{:S(2)}, u32[]{:S(2)}) collective-permute-start(f32[1,4,64,128]{3,2,1,0:T(8,128)S(1)} %get-tuple-element.1491), channel_id=1, source_target_pairs={{0,4},{4,8},{8,12},{12,16},{16,20},{20,24},{24,28},{1,5},{5,9},{9,... | collective-permute-start | bytes 393224 | tf_op jit(solution)/shard_map/ppermute | solution.py:21
  116.1 5.4 %all_gather.40 = f32[4,1,64,128]{3,2,1,0:T(8,128)S(1)} all-gather(f32[1,1,64,128]{3,2,1,0:T(8,128)S(1)} %slice.388), channel_id=1, replica_groups=mesh['strip'=8,'period'=4] {'period'}, dimensions={0}, use_global_device_ids=true | all-gather | bytes 163840 | tf_op jit(solution)/shard_map/all_gather | solution.py:26
  122.5 5.4 %all_gather.41 = f32[4,1,64,128]{3,2,1,0:T(8,128)S(1)} all-gather(f32[1,1,64,128]{3,2,1,0:T(8,128)S(1)} %slice.389), channel_id=1, replica_groups=mesh['strip'=8,'period'=4] {'period'}, dimensions={0}, use_global_device_ids=true | all-gather | bytes 163840 | tf_op jit(solution)/shard_map/all_gather | solution.py:26
  130.2 5.0 %collective-permute-start.11 = (f32[1,4,64,128]{3,2,1,0:T(8,128)S(1)}, f32[1,4,64,128]{3,2,1,0:T(8,128)S(1)}, u32[]{:S(2)}, u32[]{:S(2)}) collective-permute-start(f32[1,4,64,128]{3,2,1,0:T(8,128)S(1)} %get-tuple-element.1482), channel_id=1, source_target_pairs={{0,4},{4,8},{8,12},{12,16},{16,20},{20,24},{24,28},{1,5},{5,9},{9,... | collective-permute-start | bytes 393224 | tf_op jit(solution)/shard_map/ppermute | solution.py:45
  142.8 20.2 %all-reduce.49 = (f32[4]{0:T(128)S(1)}, f32[]{:T(128)}, f32[]{:T(128)}) all-reduce(f32[4]{0:T(128)S(1)} %convolution_bitcast_fusion.3, f32[]{:T(128)S(6)} %add.1334, f32[]{:T(128)} %get-tuple-element.1477), channel_id=1, replica_groups=mesh['strip'=8,'period'=4] {'strip'}, use_global_device_ids=true, to_apply=%region_26.27 | all-reduce | flops 6 | bytes 48 | tf_op jit(solution)/shard_map/psum | solution.py:211
  165.6 6.3 %all-reduce.52 = (f32[]{:T(128)}, f32[]{:T(128)}) all-reduce(f32[]{:T(128)S(6)} %add.1338, f32[]{:T(128)} %get-tuple-element.1434), channel_id=1, replica_groups=mesh['strip'=8,'period'=4] {'period'}, use_global_device_ids=true, to_apply=%region_28.29 | all-reduce | flops 2 | bytes 16 | tf_op jit(solution)/shard_map/psum | solution.py:226
  177.7 4.1 %collective-permute-done.13 = f32[1,4,64,128]{3,2,1,0:T(8,128)S(1)} collective-permute-done((f32[1,4,64,128]{3,2,1,0:T(8,128)S(1)}, f32[1,4,64,128]{3,2,1,0:T(8,128)S(1)}, u32[]{:S(2)}, u32[]{:S(2)}) %collective-permute-start.13) | collective-permute-done | bytes 131104 | tf_op jit(solution)/shard_map/ppermute | solution.py:21
  182.2 5.4 %all_gather.42 = f32[4,1,64,128]{3,2,1,0:T(8,128)S(1)} all-gather(f32[1,1,64,128]{3,2,1,0:T(8,128)S(1)} %slice.395), channel_id=1, replica_groups=mesh['strip'=8,'period'=4] {'period'}, dimensions={0}, use_global_device_ids=true | all-gather | bytes 163840 | tf_op jit(solution)/shard_map/all_gather | solution.py:26
  187.9 5.4 %all_gather.43 = f32[4,1,64,128]{3,2,1,0:T(8,128)S(1)} all-gather(f32[1,1,64,128]{3,2,1,0:T(8,128)S(1)} %slice.396), channel_id=1, replica_groups=mesh['strip'=8,'period'=4] {'period'}, dimensions={0}, use_global_device_ids=true | all-gather | bytes 163840 | tf_op jit(solution)/shard_map/all_gather | solution.py:26
  194.8 4.6 %collective-permute-start.15 = (f32[1,4,64,128]{3,2,1,0:T(8,128)S(1)}, f32[1,4,64,128]{3,2,1,0:T(8,128)S(1)}, u32[]{:S(2)}, u32[]{:S(2)}) collective-permute-start(f32[1,4,64,128]{3,2,1,0:T(8,128)S(1)} %broadcast_add_fusion.2), channel_id=1, source_target_pairs={{0,4},{4,8},{8,12},{12,16},{16,20},{20,24},{24,28},{1,5},{5,9},{9,... | collective-permute-start | bytes 393224 | tf_op jit(solution)/shard_map/ppermute | solution.py:45
  200.2 19.5 %psum.113 = f32[4]{0:T(128)S(1)} all-reduce(f32[4]{0:T(128)S(1)} %convolution_bitcast_fusion.2), channel_id=1, replica_groups=mesh['strip'=8,'period'=4] {'strip'}, use_global_device_ids=true, to_apply=%region_42.43 | all-reduce | flops 4 | bytes 32 | tf_op jit(solution)/shard_map/psum | solution.py:111
  221.9 4.6 %collective-permute-start.16 = (f32[1,4,64,128]{3,2,1,0:T(8,128)S(1)}, f32[1,4,64,128]{3,2,1,0:T(8,128)S(1)}, u32[]{:S(2)}, u32[]{:S(2)}) collective-permute-start(f32[1,4,64,128]{3,2,1,0:T(8,128)S(1)} %get-tuple-element.1468), channel_id=1, source_target_pairs={{0,4},{4,8},{8,12},{12,16},{16,20},{20,24},{24,28},{1,5},{5,9},{9,... | collective-permute-start | bytes 393224 | tf_op jit(solution)/shard_map/ppermute | solution.py:21
  229.3 5.4 %all_gather.44 = f32[4,1,64,128]{3,2,1,0:T(8,128)S(1)} all-gather(f32[1,1,64,128]{3,2,1,0:T(8,128)S(1)} %slice.397), channel_id=1, replica_groups=mesh['strip'=8,'period'=4] {'period'}, dimensions={0}, use_global_device_ids=true | all-gather | bytes 163840 | tf_op jit(solution)/shard_map/all_gather | solution.py:26
  235.7 5.4 %all_gather.45 = f32[4,1,64,128]{3,2,1,0:T(8,128)S(1)} all-gather(f32[1,1,64,128]{3,2,1,0:T(8,128)S(1)} %slice.398), channel_id=1, replica_groups=mesh['strip'=8,'period'=4] {'period'}, dimensions={0}, use_global_device_ids=true | all-gather | bytes 163840 | tf_op jit(solution)/shard_map/all_gather | solution.py:26
  243.4 5.6 %collective-permute-start.19 = (f32[1,4,64,128]{3,2,1,0:T(8,128)S(1)}, f32[1,4,64,128]{3,2,1,0:T(8,128)}, u32[]{:S(2)}, u32[]{:S(2)}) collective-permute-start(f32[1,4,64,128]{3,2,1,0:T(8,128)S(1)} %broadcast_add_fusion.1), channel_id=1, source_target_pairs={{0,4},{4,8},{8,12},{12,16},{16,20},{20,24},{24,28},{1,5},{5,9},{9,... | collective-permute-start | bytes 393224 | tf_op jit(solution)/shard_map/ppermute | solution.py:45
  249.1 19.6 %psum.114 = f32[4]{0:T(128)S(1)} all-reduce(f32[4]{0:T(128)S(1)} %convolution_bitcast_fusion.1), channel_id=1, replica_groups=mesh['strip'=8,'period'=4] {'strip'}, use_global_device_ids=true, to_apply=%region_49.50 | all-reduce | flops 4 | bytes 32 | tf_op jit(solution)/shard_map/psum | solution.py:111
  273.4 4.6 %collective-permute-start.20 = (f32[1,4,64,128]{3,2,1,0:T(8,128)S(1)}, f32[1,4,64,128]{3,2,1,0:T(8,128)S(1)}, u32[]{:S(2)}, u32[]{:S(2)}) collective-permute-start(f32[1,4,64,128]{3,2,1,0:T(8,128)S(1)} %get-tuple-element.1458), channel_id=1, source_target_pairs={{0,4},{4,8},{8,12},{12,16},{16,20},{20,24},{24,28},{1,5},{5,9},{9,... | collective-permute-start | bytes 393224 | tf_op jit(solution)/shard_map/ppermute | solution.py:21
  280.8 5.4 %all_gather.46 = f32[4,1,64,128]{3,2,1,0:T(8,128)S(1)} all-gather(f32[1,1,64,128]{3,2,1,0:T(8,128)S(1)} %slice.399), channel_id=1, replica_groups=mesh['strip'=8,'period'=4] {'period'}, dimensions={0}, use_global_device_ids=true | all-gather | bytes 163840 | tf_op jit(solution)/shard_map/all_gather | solution.py:26
  287.8 5.4 %all_gather.47 = f32[4,1,64,128]{3,2,1,0:T(8,128)S(1)} all-gather(f32[1,1,64,128]{3,2,1,0:T(8,128)S(1)} %slice.400), channel_id=1, replica_groups=mesh['strip'=8,'period'=4] {'period'}, dimensions={0}, use_global_device_ids=true | all-gather | bytes 163840 | tf_op jit(solution)/shard_map/all_gather | solution.py:26
  296.1 5.0 %collective-permute-start.23 = (f32[1,4,64,128]{3,2,1,0:T(8,128)S(1)}, f32[1,4,64,128]{3,2,1,0:T(8,128)S(1)}, u32[]{:S(2)}, u32[]{:S(2)}) collective-permute-start(f32[1,4,64,128]{3,2,1,0:T(8,128)S(1)} %get-tuple-element.1448), channel_id=1, source_target_pairs={{0,4},{4,8},{8,12},{12,16},{16,20},{20,24},{24,28},{1,5},{5,9},{9,... | collective-permute-start | bytes 393224 | tf_op jit(solution)/shard_map/ppermute | solution.py:45
  309.5 20.2 %all-reduce.48 = (f32[4]{0:T(128)S(1)}, f32[]{:T(128)}, f32[]{:T(128)}) all-reduce(f32[4]{0:T(128)S(1)} %convolution_bitcast_fusion, f32[]{:T(128)S(6)} %add.1394, f32[]{:T(128)} %get-tuple-element.1443), channel_id=1, replica_groups=mesh['strip'=8,'period'=4] {'strip'}, use_global_device_ids=true, to_apply=%region_53.54 | all-reduce | flops 6 | bytes 48 | tf_op jit(solution)/shard_map/psum | solution.py:211
  332.7 6.2 %all-reduce.51 = (f32[]{:T(128)}, f32[]{:T(128)}) all-reduce(f32[]{:T(128)S(6)} %add.1395, f32[]{:T(128)} %get-tuple-element.1431), channel_id=1, replica_groups=mesh['strip'=8,'period'=4] {'period'}, use_global_device_ids=true, to_apply=%region_58.59 | all-reduce | flops 2 | bytes 16 | tf_op jit(solution)/shard_map/psum | solution.py:226
  (254 shorter events, 75.0 us)
Async XLA Ops:
  3.1 8.6 %collective-permute-start = (f32[1,4,64,128]{3,2,1,0:T(8,128)S(1)}, f32[1,4,64,128]{3,2,1,0:T(8,128)S(1)}, u32[]{:S(2)}, u32[]{:S(2)}) collective-permute-start(f32[1,4,64,128]{3,2,1,0:T(8,128)S(1)} %get-tuple-element.1518), channel_id=1, source_target_pairs={{0,4},{4,8},{8,12},{12,16},{16,20},{20,24},{24,28},{1,5},{5,9},{9,... | collective-permute-start | bytes 393224 | tf_op jit(solution)/shard_map/ppermute | solution.py:21
  8.0 1.4 copy-start.10
  8.0 6.9 %collective-permute-start.1 = (f32[1,4,64,128]{3,2,1,0:T(8,128)S(1)}, f32[1,4,64,128]{3,2,1,0:T(8,128)S(1)}, u32[]{:S(2)}, u32[]{:S(2)}) collective-permute-start(f32[1,4,64,128]{3,2,1,0:T(8,128)S(1)} %get-tuple-element.1517), channel_id=1, source_target_pairs={{4,0},{8,4},{12,8},{16,12},{20,16},{24,20},{28,24},{5,1},{9,5},{13... | collective-permute-start | bytes 393224 | tf_op jit(solution)/shard_map/ppermute | solution.py:21
  10.0 4.8 %copy-start = (f32[1,4,64,128]{3,2,1,0:T(8,128)S(1)}, f32[1,4,64,128]{3,2,1,0:T(8,128)}, u32[]{:S(2)}) copy-start(f32[1,4,64,128]{3,2,1,0:T(8,128)} %param.36) | copy-start | bytes 393220
  15.2 5.6 %copy-start.2 = (f32[1,64,128]{2,1,0:T(8,128)S(1)}, f32[1,64,128]{2,1,0:T(8,128)}, u32[]{:S(2)}) copy-start(f32[1,64,128]{2,1,0:T(8,128)} %param.39) | copy-start | bytes 98308
  27.2 29.3 %collective-permute-start.2 = (f32[1,4,64,128]{3,2,1,0:T(8,128)S(1)}, f32[1,4,64,128]{3,2,1,0:T(8,128)S(1)}, u32[]{:S(2)}, u32[]{:S(2)}) collective-permute-start(f32[1,4,64,128]{3,2,1,0:T(8,128)S(1)} %broadcast_add_fusion.5), channel_id=1, source_target_pairs={{4,0},{8,4},{12,8},{16,12},{20,16},{24,20},{28,24},{5,1},{9,5},{13... | collective-permute-start | bytes 393224 | tf_op jit(solution)/shard_map/ppermute | solution.py:46
  28.5 28.1 %collective-permute-start.3 = (f32[1,4,64,128]{3,2,1,0:T(8,128)S(1)}, f32[1,4,64,128]{3,2,1,0:T(8,128)S(1)}, u32[]{:S(2)}, u32[]{:S(2)}) collective-permute-start(f32[1,4,64,128]{3,2,1,0:T(8,128)S(1)} %broadcast_add_fusion.5), channel_id=1, source_target_pairs={{0,4},{4,8},{8,12},{12,16},{16,20},{20,24},{24,28},{1,5},{5,9},{9,... | collective-permute-start | bytes 393224 | tf_op jit(solution)/shard_map/ppermute | solution.py:45
  56.7 5.9 %copy-start.4 = (f32[5,1,4,64,128]{4,3,2,1,0:T(8,128)}, f32[5,1,4,64,128]{4,3,2,1,0:T(8,128)S(1)}, u32[]{:S(2)}) copy-start(f32[5,1,4,64,128]{4,3,2,1,0:T(8,128)S(1)} %get-tuple-element.1498) | copy-start | bytes 1966084
  56.8 7.4 %collective-permute-start.5 = (f32[1,4,64,128]{3,2,1,0:T(8,128)S(1)}, f32[1,4,64,128]{3,2,1,0:T(8,128)S(1)}, u32[]{:S(2)}, u32[]{:S(2)}) collective-permute-start(f32[1,4,64,128]{3,2,1,0:T(8,128)S(1)} %get-tuple-element.1499), channel_id=1, source_target_pairs={{4,0},{8,4},{12,8},{16,12},{20,16},{24,20},{28,24},{5,1},{9,5},{13... | collective-permute-start | bytes 393224 | tf_op jit(solution)/shard_map/ppermute | solution.py:21
  58.1 7.1 %collective-permute-start.4 = (f32[1,4,64,128]{3,2,1,0:T(8,128)S(1)}, f32[1,4,64,128]{3,2,1,0:T(8,128)S(1)}, u32[]{:S(2)}, u32[]{:S(2)}) collective-permute-start(f32[1,4,64,128]{3,2,1,0:T(8,128)S(1)} %get-tuple-element.1501), channel_id=1, source_target_pairs={{0,4},{4,8},{8,12},{12,16},{16,20},{20,24},{24,28},{1,5},{5,9},{9,... | collective-permute-start | bytes 393224 | tf_op jit(solution)/shard_map/ppermute | solution.py:21
  77.5 27.6 %collective-permute-start.6 = (f32[1,4,64,128]{3,2,1,0:T(8,128)S(1)}, f32[1,4,64,128]{3,2,1,0:T(8,128)S(1)}, u32[]{:S(2)}, u32[]{:S(2)}) collective-permute-start(f32[1,4,64,128]{3,2,1,0:T(8,128)S(1)} %broadcast_add_fusion.4), channel_id=1, source_target_pairs={{4,0},{8,4},{12,8},{16,12},{20,16},{24,20},{28,24},{5,1},{9,5},{13... | collective-permute-start | bytes 393224 | tf_op jit(solution)/shard_map/ppermute | solution.py:46
  79.5 26.4 %collective-permute-start.7 = (f32[1,4,64,128]{3,2,1,0:T(8,128)S(1)}, f32[1,4,64,128]{3,2,1,0:T(8,128)S(1)}, u32[]{:S(2)}, u32[]{:S(2)}) collective-permute-start(f32[1,4,64,128]{3,2,1,0:T(8,128)S(1)} %broadcast_add_fusion.4), channel_id=1, source_target_pairs={{0,4},{4,8},{8,12},{12,16},{16,20},{20,24},{24,28},{1,5},{5,9},{9,... | collective-permute-start | bytes 393224 | tf_op jit(solution)/shard_map/ppermute | solution.py:45
  107.5 6.8 %collective-permute-start.9 = (f32[1,4,64,128]{3,2,1,0:T(8,128)S(1)}, f32[1,4,64,128]{3,2,1,0:T(8,128)S(1)}, u32[]{:S(2)}, u32[]{:S(2)}) collective-permute-start(f32[1,4,64,128]{3,2,1,0:T(8,128)S(1)} %get-tuple-element.1489), channel_id=1, source_target_pairs={{4,0},{8,4},{12,8},{16,12},{20,16},{24,20},{28,24},{5,1},{9,5},{13... | collective-permute-start | bytes 393224 | tf_op jit(solution)/shard_map/ppermute | solution.py:21
  108.7 7.1 %collective-permute-start.8 = (f32[1,4,64,128]{3,2,1,0:T(8,128)S(1)}, f32[1,4,64,128]{3,2,1,0:T(8,128)S(1)}, u32[]{:S(2)}, u32[]{:S(2)}) collective-permute-start(f32[1,4,64,128]{3,2,1,0:T(8,128)S(1)} %get-tuple-element.1491), channel_id=1, source_target_pairs={{0,4},{4,8},{8,12},{12,16},{16,20},{20,24},{24,28},{1,5},{5,9},{9,... | collective-permute-start | bytes 393224 | tf_op jit(solution)/shard_map/ppermute | solution.py:21
  128.9 8.4 %collective-permute-start.10 = (f32[1,4,64,128]{3,2,1,0:T(8,128)S(1)}, f32[1,4,64,128]{3,2,1,0:T(8,128)S(1)}, u32[]{:S(2)}, u32[]{:S(2)}) collective-permute-start(f32[1,4,64,128]{3,2,1,0:T(8,128)S(1)} %get-tuple-element.1482), channel_id=1, source_target_pairs={{4,0},{8,4},{12,8},{16,12},{20,16},{24,20},{28,24},{5,1},{9,5},{13... | collective-permute-start | bytes 393224 | tf_op jit(solution)/shard_map/ppermute | solution.py:46
  130.2 10.0 %collective-permute-start.11 = (f32[1,4,64,128]{3,2,1,0:T(8,128)S(1)}, f32[1,4,64,128]{3,2,1,0:T(8,128)S(1)}, u32[]{:S(2)}, u32[]{:S(2)}) collective-permute-start(f32[1,4,64,128]{3,2,1,0:T(8,128)S(1)} %get-tuple-element.1482), channel_id=1, source_target_pairs={{0,4},{4,8},{8,12},{12,16},{16,20},{20,24},{24,28},{1,5},{5,9},{9,... | collective-permute-start | bytes 393224 | tf_op jit(solution)/shard_map/ppermute | solution.py:45
  137.4 3.2 copy-start.3
  137.4 3.2 copy-start.5
  173.4 4.3 %collective-permute-start.12 = (f32[1,4,64,128]{3,2,1,0:T(8,128)S(1)}, f32[1,4,64,128]{3,2,1,0:T(8,128)S(1)}, u32[]{:S(2)}, u32[]{:S(2)}) collective-permute-start(f32[1,4,64,128]{3,2,1,0:T(8,128)S(1)} %get-tuple-element.1513), channel_id=1, source_target_pairs={{0,4},{4,8},{8,12},{12,16},{16,20},{20,24},{24,28},{1,5},{5,9},{9,... | collective-permute-start | bytes 393224 | tf_op jit(solution)/shard_map/ppermute | solution.py:21
  174.9 7.0 %collective-permute-start.13 = (f32[1,4,64,128]{3,2,1,0:T(8,128)S(1)}, f32[1,4,64,128]{3,2,1,0:T(8,128)S(1)}, u32[]{:S(2)}, u32[]{:S(2)}) collective-permute-start(f32[1,4,64,128]{3,2,1,0:T(8,128)S(1)} %get-tuple-element.1512), channel_id=1, source_target_pairs={{4,0},{8,4},{12,8},{16,12},{20,16},{24,20},{28,24},{5,1},{9,5},{13... | collective-permute-start | bytes 393224 | tf_op jit(solution)/shard_map/ppermute | solution.py:21
  193.5 26.8 %collective-permute-start.14 = (f32[1,4,64,128]{3,2,1,0:T(8,128)S(1)}, f32[1,4,64,128]{3,2,1,0:T(8,128)S(1)}, u32[]{:S(2)}, u32[]{:S(2)}) collective-permute-start(f32[1,4,64,128]{3,2,1,0:T(8,128)S(1)} %broadcast_add_fusion.2), channel_id=1, source_target_pairs={{4,0},{8,4},{12,8},{16,12},{20,16},{24,20},{28,24},{5,1},{9,5},{13... | collective-permute-start | bytes 393224 | tf_op jit(solution)/shard_map/ppermute | solution.py:46
  194.8 25.6 %collective-permute-start.15 = (f32[1,4,64,128]{3,2,1,0:T(8,128)S(1)}, f32[1,4,64,128]{3,2,1,0:T(8,128)S(1)}, u32[]{:S(2)}, u32[]{:S(2)}) collective-permute-start(f32[1,4,64,128]{3,2,1,0:T(8,128)S(1)} %broadcast_add_fusion.2), channel_id=1, source_target_pairs={{0,4},{4,8},{8,12},{12,16},{16,20},{20,24},{24,28},{1,5},{5,9},{9,... | collective-permute-start | bytes 393224 | tf_op jit(solution)/shard_map/ppermute | solution.py:45
  220.6 6.9 %collective-permute-start.17 = (f32[1,4,64,128]{3,2,1,0:T(8,128)S(1)}, f32[1,4,64,128]{3,2,1,0:T(8,128)S(1)}, u32[]{:S(2)}, u32[]{:S(2)}) collective-permute-start(f32[1,4,64,128]{3,2,1,0:T(8,128)S(1)} %get-tuple-element.1466), channel_id=1, source_target_pairs={{4,0},{8,4},{12,8},{16,12},{20,16},{24,20},{28,24},{5,1},{9,5},{13... | collective-permute-start | bytes 393224 | tf_op jit(solution)/shard_map/ppermute | solution.py:21
  221.9 7.1 %collective-permute-start.16 = (f32[1,4,64,128]{3,2,1,0:T(8,128)S(1)}, f32[1,4,64,128]{3,2,1,0:T(8,128)S(1)}, u32[]{:S(2)}, u32[]{:S(2)}) collective-permute-start(f32[1,4,64,128]{3,2,1,0:T(8,128)S(1)} %get-tuple-element.1468), channel_id=1, source_target_pairs={{0,4},{4,8},{8,12},{12,16},{16,20},{20,24},{24,28},{1,5},{5,9},{9,... | collective-permute-start | bytes 393224 | tf_op jit(solution)/shard_map/ppermute | solution.py:21
  226.6 2.5 copy-start.6
  241.4 27.9 %collective-permute-start.18 = (f32[1,4,64,128]{3,2,1,0:T(8,128)S(1)}, f32[1,4,64,128]{3,2,1,0:T(8,128)S(1)}, u32[]{:S(2)}, u32[]{:S(2)}) collective-permute-start(f32[1,4,64,128]{3,2,1,0:T(8,128)S(1)} %broadcast_add_fusion.1), channel_id=1, source_target_pairs={{4,0},{8,4},{12,8},{16,12},{20,16},{24,20},{28,24},{5,1},{9,5},{13... | collective-permute-start | bytes 393224 | tf_op jit(solution)/shard_map/ppermute | solution.py:46
  243.4 27.5 %collective-permute-start.19 = (f32[1,4,64,128]{3,2,1,0:T(8,128)S(1)}, f32[1,4,64,128]{3,2,1,0:T(8,128)}, u32[]{:S(2)}, u32[]{:S(2)}) collective-permute-start(f32[1,4,64,128]{3,2,1,0:T(8,128)S(1)} %broadcast_add_fusion.1), channel_id=1, source_target_pairs={{0,4},{4,8},{8,12},{12,16},{16,20},{20,24},{24,28},{1,5},{5,9},{9,... | collective-permute-start | bytes 393224 | tf_op jit(solution)/shard_map/ppermute | solution.py:45
  272.1 6.9 %collective-permute-start.21 = (f32[1,4,64,128]{3,2,1,0:T(8,128)S(1)}, f32[1,4,64,128]{3,2,1,0:T(8,128)S(1)}, u32[]{:S(2)}, u32[]{:S(2)}) collective-permute-start(f32[1,4,64,128]{3,2,1,0:T(8,128)S(1)} %get-tuple-element.1456), channel_id=1, source_target_pairs={{4,0},{8,4},{12,8},{16,12},{20,16},{24,20},{28,24},{5,1},{9,5},{13... | collective-permute-start | bytes 393224 | tf_op jit(solution)/shard_map/ppermute | solution.py:21
  273.4 7.1 %collective-permute-start.20 = (f32[1,4,64,128]{3,2,1,0:T(8,128)S(1)}, f32[1,4,64,128]{3,2,1,0:T(8,128)S(1)}, u32[]{:S(2)}, u32[]{:S(2)}) collective-permute-start(f32[1,4,64,128]{3,2,1,0:T(8,128)S(1)} %get-tuple-element.1458), channel_id=1, source_target_pairs={{0,4},{4,8},{8,12},{12,16},{16,20},{20,24},{24,28},{1,5},{5,9},{9,... | collective-permute-start | bytes 393224 | tf_op jit(solution)/shard_map/ppermute | solution.py:21
  294.8 8.4 %collective-permute-start.22 = (f32[1,4,64,128]{3,2,1,0:T(8,128)S(1)}, f32[1,4,64,128]{3,2,1,0:T(8,128)S(1)}, u32[]{:S(2)}, u32[]{:S(2)}) collective-permute-start(f32[1,4,64,128]{3,2,1,0:T(8,128)S(1)} %get-tuple-element.1448), channel_id=1, source_target_pairs={{4,0},{8,4},{12,8},{16,12},{20,16},{24,20},{28,24},{5,1},{9,5},{13... | collective-permute-start | bytes 393224 | tf_op jit(solution)/shard_map/ppermute | solution.py:46
  296.1 10.0 %collective-permute-start.23 = (f32[1,4,64,128]{3,2,1,0:T(8,128)S(1)}, f32[1,4,64,128]{3,2,1,0:T(8,128)S(1)}, u32[]{:S(2)}, u32[]{:S(2)}) collective-permute-start(f32[1,4,64,128]{3,2,1,0:T(8,128)S(1)} %get-tuple-element.1448), channel_id=1, source_target_pairs={{0,4},{4,8},{8,12},{12,16},{16,20},{20,24},{24,28},{1,5},{5,9},{9,... | collective-permute-start | bytes 393224 | tf_op jit(solution)/shard_map/ppermute | solution.py:45
  303.3 3.2 copy-start.7
  (7 other events, 5.7 us)
where the time goes:
time: 343 us; the launch traced here: 341 us
  blocking collectives  198 us (58%)
  starting transfers between devices  70.2 us (20%)
  other arithmetic  28 us (8%)
  waiting for transfers between devices  24.6 us (7%)
  between operations  11.5 us (3%)
  matrix products  4.41 us (1%)
  local copies, waits for them, and re-layouts  3.57 us (1%)
    psum x4, blocking collectives, capacity_sum(): return lax.psum(row_local, 'strip')  80 us
    all_gather x12, blocking collectives, carried_in(): everything = lax.all_gather(value, axis)  65 us
    psum x2, blocking collectives, per_device(): lax.psum((row_local, move_primal, move_dual), 'strip')  40.5 us
    ppermute x12, starting transfers between devices, from_behind(): return lax.ppermute(value, axis, pairs)  32.3 us
    ppermute x6, starting transfers between devices, padded_2(): before = lax.ppermute(last, axis, up)  30.1 us
    ppermute x12, waiting for transfers between devices, from_behind(): return lax.ppermute(value, axis, pairs)  16.1 us
    psum x2, blocking collectives, per_device(): lax.psum((move_primal, move_dual + move_cap), 'period')  12.5 us
    unnamed x40, other arithmetic  7.87 us
  transfers between devices with their start and end apart: 24, of which 14 were waited for; matrix products, arithmetic and copies ran while one was open for 4% of the time, Pallas kernels for 0%

commit v1 on v0

v1 whole, which is shorter than its diff:
```python
import functools
import math

import jax
import jax.numpy as jnp
from jax import lax
from jax.experimental import pallas as pl
from jax.experimental.pallas import tpu as pltpu
from jax.sharding import PartitionSpec as P

OUTER = 2
INNER = 3
STEPS = OUTER * INNER
RATE = math.log(1.1) / 12.0
EPS = 1e-06
SLOPE = 11.0
MESH = pl.DeviceIdType.MESH


def kernel(
    NS, NPD, T, Z, Y, R,
    u_ref, prec_ref, bound_ref, cap_ref, capacity_ref, bv_ref, tc_ref, dens_ref, slope_ref, om_ref,
    u_out, prec_out, bound_out, cap_out, w_out,
    uf, uc, us, bf, bc, bs, fa, ca, sa, act, ton, tb, tl, cb, ex0,
    xs, xr, es, er, as_, ar, rs, rb, ps, pb, slr,
    ini_s, ini_r, xs_s, xs_r, e_s, e_r, a_s, a_r, r_s, r_r, p_s, p_r,
):
    me = lax.axis_index("strip")
    pe = lax.axis_index("period")
    total_rows = NS
    total_periods = NPD * T
    blocks_all = float(total_rows * Z * Y)
    root_blocks = math.sqrt(blocks_all)
    sends = []

    barrier = pltpu.get_barrier_semaphore()
    for k in range(1, NS):
        pl.semaphore_signal(barrier, inc=1, device_id={"strip": lax.rem(me + k, NS)}, device_id_type=MESH)
    for k in range(1, NPD):
        pl.semaphore_signal(barrier, inc=1, device_id={"period": lax.rem(pe + k, NPD)}, device_id_type=MESH)
    pl.semaphore_wait(barrier, NS + NPD - 2)

    has = (me < NS - 1, me > 0)
    gets = (me > 0, me < NS - 1)
    to = (me + 1, me - 1)

    def remote(src, dst, ss, rr, dev):
        return pltpu.make_async_remote_copy(
            src_ref=src, dst_ref=dst, send_sem=ss, recv_sem=rr, device_id=dev, device_id_type=MESH
        )

    def ini_copy(d, what):
        if what == 0:
            return remote(prec_ref.at[1 + d, 0], fa.at[5 + d], ini_s.at[d, 0], ini_r.at[d, 0], {"strip": to[d]})
        return remote(slope_ref, slr.at[d], ini_s.at[d, 1], ini_r.at[d, 1], {"strip": to[d]})

    def x_copy(d, part, s):
        lo, size = (1, T - 1) if part == 0 else (0, 1)
        return remote(
            xs.at[s, pl.ds(lo, size)], xr.at[d, s, pl.ds(lo, size)],
            xs_s.at[d, part, s], xs_r.at[d, part, s], {"strip": to[d]},
        )

    def e_copy(k, s):
        return remote(es.at[s], er.at[s, k - 1], e_s.at[s, k - 1], e_r.at[s, k - 1], {"period": pe + k})

    def a_copy(k, s):
        return remote(as_.at[s], ar.at[s, k - 1], a_s.at[s, k - 1], a_r.at[s, k - 1], {"period": pe - k})

    def r_copy(k, slot):
        return remote(
            rs.at[slot], rb.at[slot, me], r_s.at[slot, k - 1], r_r.at[slot, k - 1],
            {"strip": lax.rem(me + k, NS)},
        )

    def p_copy(k, slot):
        return remote(
            ps.at[slot], pb.at[slot, pe], p_s.at[slot, k - 1], p_r.at[slot, k - 1],
            {"period": lax.rem(pe + k, NPD)},
        )

    def start(cond, copy):
        def go():
            copy.start()
        if cond is None:
            go()
        else:
            pl.when(cond)(go)
        sends.append((cond, copy))

    def wait_recv(cond, copy):
        if cond is None:
            copy.wait_recv()
        else:
            pl.when(cond)(lambda: copy.wait_recv())

    def reduce_start(slot, value):
        rs[slot] = value
        rb[slot, me] = value
        for k in range(1, NS):
            start(None, r_copy(k, slot))

    def reduce_done(slot):
        for k in range(1, NS):
            wait_recv(None, r_copy(k, slot))
        total = rb[slot, 0]
        for k in range(1, NS):
            total = total + rb[slot, k]
        return total

    for d in range(2):
        start(has[d], ini_copy(d, 1))
        start(has[d], ini_copy(d, 0))

    def fold(v):
        return jnp.sum(v.reshape(Z // 8, 8, Y), axis=0)

    cls = tc_ref[0]
    tons = jnp.zeros((Z, Y), jnp.float32)
    for c in range(dens_ref.shape[0]):
        tons = jnp.where(cls == c, (1.0 + c) * dens_ref[c], tons)
    ton[...] = tons
    rows = lax.broadcasted_iota(jnp.int32, (R, Y), 0)
    part = jnp.sum(tons, axis=0, keepdims=True)
    reduce_start(0, jnp.where(rows == 0, part, 0.0))

    z_ids = lax.broadcasted_iota(jnp.int32, (Z, Y), 0)
    y_ids = lax.broadcasted_iota(jnp.int32, (Z, Y), 1)

    def mask_of(codes, k, inside):
        ok = z_ids >= 1
        if k > 0:
            ok = ok & (jnp.broadcast_to((codes >> (k - 1)) & 1, (Z, Y)) == 1)
        if k == 3:
            ok = ok & (y_ids < Y - 1)
        if k == 4:
            ok = ok & (y_ids >= 1)
        if inside is not None:
            ok = ok & (jnp.full((Z, Y), inside.astype(jnp.int32)) == 1)
        return ok.astype(jnp.float32)

    own = slope_ref[...]
    act[0] = mask_of(own, 0, None)
    act[1] = mask_of(own, 1, me < NS - 1)
    act[2] = mask_of(own, 2, me > 0)
    act[3] = mask_of(own, 3, None)
    act[4] = mask_of(own, 4, None)

    period = [(pe * T + t).astype(jnp.float32) for t in range(T)]
    pid = [jnp.full((1, Y), period[t]) for t in range(T)]
    disc = [jnp.exp(-RATE * pid[t]) for t in range(T)]
    tonr = ton[...] * (1.0 / root_blocks)
    for t in range(T):
        tb[t] = 1.0 / (SLOPE * (total_periods - pid[t]) + tonr)
        uf[t] = u_ref[0, t]
        bf[t] = bound_ref[0, t]
        for k in range(5):
            fa[k, t] = prec_ref[k, 0, t] * act[k]

    caps = jnp.zeros((R, Y), jnp.float32)
    climit = jnp.zeros((R, Y), jnp.float32)
    for t in range(T):
        caps = jnp.where(rows == t, cap_ref[t], caps)
        climit = jnp.where(rows == t, capacity_ref[t] * blocks_all, climit)
    w = jnp.full((1, Y), om_ref[0])

    for d in range(2):
        @pl.when(jnp.logical_not(gets[d]))
        def _():
            act[5 + d] = jnp.zeros((Z, Y), jnp.float32)
            fa[5 + d] = jnp.zeros((T, Z, Y), jnp.float32)
            for s in range(STEPS):
                xr[d, s] = jnp.zeros((T, Z, Y), jnp.float32)

        wait_recv(gets[d], ini_copy(d, 1))
        wait_recv(gets[d], ini_copy(d, 0))

        @pl.when(gets[d])
        def _():
            act[5 + d] = mask_of(slr[d], 1 + d, None)
            for t in range(T):
                fa[5 + d, t] = fa[5 + d, t] * act[5 + d]

    def up_y(v):
        return pltpu.roll(v, 1, 1)

    def dn_y(v):
        return pltpu.roll(v, Y - 1, 1)

    def up_z(v):
        return pltpu.roll(v, 1, 0)

    def dn_z(v):
        return pltpu.roll(v, Z - 1, 0)

    def settle(first, cur, acc, at, j, new, old):
        if j == 0:
            cur[at] = new
            return new, None
        if j == 1:
            cur[at] = new
            acc[at] = old + new
            return new, None
        mean = (acc[at] + new) * (1.0 / INNER)
        diff = mean - first[at]
        first[at] = mean
        return mean, fold(diff * diff)

    def gradient(s, arcs, bounds):
        tail = None
        for t in range(T - 1, -1, -1):
            p = [arcs[k, t] for k in range(5)]
            g = (((p[0] + p[1]) + (p[2] + p[3])) + p[4]) + bounds[t]
            back = ((p[0] + arcs[5, t]) + arcs[6, t]) + (up_y(p[3]) + dn_y(p[4]))
            g = g - dn_z(back)
            tail = g if tail is None else tail + g
            tl[t] = tail
        as_[s] = tail
        for k in range(1, NPD):
            start(pe >= k, a_copy(k, s))

    gradient(0, fa, bf)
    tons_all = jnp.sum(jnp.sum(reduce_done(0), axis=0, keepdims=True), axis=1, keepdims=True)
    inv_tons = 1.0 / tons_all
    cap_first = cap_sum = None

    for s in range(STEPS):
        j = s % INNER
        u_src = uf if j == 0 else uc
        b_src = bf if j == 0 else bc
        p_src = fa if j == 0 else ca
        inv_w = 1.0 / w
        move_p = jnp.zeros((8, Y), jnp.float32)
        move_d = jnp.zeros((8, Y), jnp.float32)
        for k in range(1, NPD):
            @pl.when(pe + k < NPD)
            def _():
                a_copy(k, s).wait_recv()
                for t in range(T):
                    tl[t] = tl[t] + ar[s, k - 1]
        head = None
        row = jnp.zeros((R, Y), jnp.float32)
        for t in range(T):
            old = u_src[t]
            grad = tl[t] + (ton[...] * (1.0 / root_blocks)) * caps[t : t + 1, :]
            new = jnp.maximum(old - (tb[t] * inv_w) * (grad - bv_ref[0] * disc[t]), 0.0)
            ext = 2.0 * new - old
            _, moved = settle(uf, uc, us, t, j, new, old)
            if moved is not None:
                move_p = move_p + moved
            if t == 0:
                ex0[...] = ext
            else:
                xs[s, t] = ext
            head = ext if head is None else head + ext
            row = jnp.where(rows == t, jnp.sum(ton[...] * ext, axis=0, keepdims=True), row)
        es[s] = head
        for k in range(1, NPD):
            start(pe + k < NPD, e_copy(k, s))
        for d in range(2):
            start(has[d], x_copy(d, 0, s))
        reduce_start(1 + s, row)
        for k in range(1, NPD):
            @pl.when(pe >= k)
            def _():
                e_copy(k, s).wait_recv()
                ex0[...] = ex0[...] + er[s, k - 1]
        xs[s, 0] = ex0[...]
        for d in range(2):
            start(has[d], x_copy(d, 1, s))
        total = None
        for t in range(T):
            total = xs[s, t] if t == 0 else total + xs[s, t]
            cb[t] = total
        rate_b = [w / (pid[t] + 1.0) for t in range(T)]
        rate_p = [w / (2.0 * (pid[t] + 1.0)) for t in range(T)]

        def arc(k, t, diff, move):
            old = p_src[k, t]
            new = jnp.maximum(old + rate_p[t] * diff, 0.0) * act[k]
            _, moved = settle(fa, ca, sa, (k, t), j, new, old)
            if moved is not None and k < 5:
                move = move + moved
            return move

        for t in range(T):
            c = cb[t]
            old = b_src[t]
            new = jnp.maximum(old + rate_b[t] * (c - 1.0), 0.0)
            _, moved = settle(bf, bc, bs, t, j, new, old)
            if moved is not None:
                move_d = move_d + moved
            cz = up_z(c)
            move_d = arc(0, t, c - cz, move_d)
            move_d = arc(3, t, c - dn_y(cz), move_d)
            move_d = arc(4, t, c - up_y(cz), move_d)
        for part in range(2):
            for d in range(2):
                wait_recv(gets[d], x_copy(d, part, s))
        total_m = total_p = None
        for t in range(T):
            total_m = xr[0, s, t] if t == 0 else total_m + xr[0, s, t]
            total_p = xr[1, s, t] if t == 0 else total_p + xr[1, s, t]
            c = cb[t]
            cz = up_z(c)
            move_d = arc(1, t, c - up_z(total_p), move_d)
            move_d = arc(2, t, c - up_z(total_m), move_d)
            move_d = arc(5, t, total_m - cz, move_d)
            move_d = arc(6, t, total_p - cz, move_d)
        last = j == INNER - 1
        if s < STEPS - 1:
            gradient(s + 1, fa if last else ca, bf if last else bc)
        if last:
            cyc = s // INNER
            mp = jnp.sum(move_p, axis=0, keepdims=True)
            md = jnp.sum(move_d, axis=0, keepdims=True)
            reduce_start(1 + STEPS + cyc, jnp.where(rows == 0, mp, jnp.where(rows == 1, md, 0.0)))
        row_total = jnp.sum(reduce_done(1 + s), axis=1, keepdims=True)
        new_caps = jnp.maximum(caps + w * ((row_total - climit) * inv_tons), 0.0)
        new_caps = jnp.where(rows < T, new_caps, 0.0)
        if j == 0:
            cap_first = caps
            cap_sum = new_caps
        else:
            cap_sum = cap_sum + new_caps
        caps = new_caps
        if last:
            caps = cap_sum * (1.0 / INNER)
            cap_move = jnp.sum((caps - cap_first) ** 2, axis=0, keepdims=True)
            got = jnp.sum(reduce_done(1 + STEPS + cyc), axis=1, keepdims=True)
            msg = jnp.broadcast_to(got, (R, Y)) + jnp.where(rows == 1, cap_move, 0.0)
            ps[cyc] = msg
            pb[cyc, pe] = msg
            for k in range(1, NPD):
                start(None, p_copy(k, cyc))
            if s == STEPS - 1:
                for t in range(T):
                    u_out[0, t] = uf[t]
                    bound_out[0, t] = bf[t]
                    for k in range(5):
                        prec_out[k, 0, t] = fa[k, t]
                    cap_out[t] = caps[t, 0]
            for k in range(1, NPD):
                wait_recv(None, p_copy(k, cyc))
            tot = pb[cyc, 0]
            for k in range(1, NPD):
                tot = tot + pb[cyc, k]
            w = jnp.sqrt(w * jnp.sqrt((tot[1:2, :] + EPS) / (tot[0:1, :] + EPS)))
    w_out[0] = w[0, 0]
    for cond, copy in sends:
        if cond is None:
            copy.wait_send()
        else:
            pl.when(cond)(lambda copy=copy: copy.wait_send())


def solution(mesh):
    NS, NPD = mesh.shape["strip"], mesh.shape["period"]

    def per_device(u, prec, bound, cap, capacity, bv, tc, dens, slope, om):
        rows_here, T, Z, Y = u.shape
        assert rows_here == 1
        R = -(-T // 8) * 8
        f32 = jnp.float32
        vmem = pl.BlockSpec(memory_space=pltpu.VMEM)
        smem = pl.BlockSpec(memory_space=pltpu.SMEM)
        plane = lambda *n: pltpu.VMEM((*n, Z, Y), f32)
        dma = pltpu.SemaphoreType.DMA
        slots = 1 + STEPS + OUTER
        far = max(NPD - 1, 1)
        return pl.pallas_call(
            functools.partial(kernel, NS, NPD, T, Z, Y, R),
            out_shape=(
                jax.ShapeDtypeStruct(u.shape, f32),
                jax.ShapeDtypeStruct(prec.shape, f32),
                jax.ShapeDtypeStruct(bound.shape, f32),
                jax.ShapeDtypeStruct(cap.shape, f32),
                jax.ShapeDtypeStruct((1,), f32),
            ),
            in_specs=[vmem, vmem, vmem, smem, smem, vmem, vmem, smem, vmem, smem],
            out_specs=(vmem, vmem, vmem, smem, smem),
            scratch_shapes=[
                plane(T), plane(T), plane(T), plane(T), plane(T), plane(T),
                plane(7, T), plane(7, T), plane(7, T), plane(7), plane(), plane(T), plane(T), plane(T), plane(),
                plane(STEPS, T), plane(2, STEPS, T), plane(STEPS), plane(STEPS, far),
                plane(STEPS), plane(STEPS, far),
                pltpu.VMEM((slots, R, Y), f32), pltpu.VMEM((slots, NS, R, Y), f32),
                pltpu.VMEM((OUTER, R, Y), f32), pltpu.VMEM((OUTER, NPD, R, Y), f32),
                pltpu.VMEM((2, 1, Y), jnp.int32),
                dma((2, 2)), dma((2, 2)), dma((2, 2, STEPS)), dma((2, 2, STEPS)),
                dma((STEPS, far)), dma((STEPS, far)), dma((STEPS, far)), dma((STEPS, far)),
                dma((slots, NS - 1)), dma((slots, NS - 1)), dma((OUTER, far)), dma((OUTER, far)),
            ],
            compiler_params=pltpu.CompilerParams(collective_id=0, has_side_effects=True),
        )(u, prec, bound, cap, capacity, bv, tc, dens, slope, om)

    in_specs = (
        P("strip", "period", None, None),
        P(None, "strip", "period", None, None),
        P("strip", "period", None, None),
        P("period"),
        P("period"),
        P("strip", None, None),
        P("strip", None, None),
        P(),
        P("strip", None),
        P(),
    )
    out_specs = (
        P("strip", "period", None, None),
        P(None, "strip", "period", None, None),
        P("strip", "period", None, None),
        P("period"),
        P(),
    )
    return jax.shard_map(
        per_device, mesh=mesh, in_specs=in_specs, out_specs=out_specs, check_vma=False
    )
```

time: 343 us -> 98.1 us (0.29)
  blocking collectives: 198 us -> 0 us
  Pallas kernels: 0 us -> 90 us
  starting transfers between devices: 70.2 us -> 0 us
  other arithmetic: 28 us -> 0 us
  waiting for transfers between devices: 24.6 us -> 0 us
  between operations: 11.5 us -> 3.1 us
  matrix products: 4.41 us -> 0 us
    psum x8 -> x0, blocking collectives: 133 us -> none  [the longest x4 80 us: capacity_sum(): return lax.psum(row_local, 'strip')]
    pallas_call x0 -> x1, Pallas kernels: none -> 90 us  [per_device(): pl.pallas_call(functools.partial(kernel, NS, NPD, T, Z, Y, R), out_shape=...]
    ppermute x24 -> x0, starting transfers between devices: 70.2 us -> none  [the longest x12 32.3 us: from_behind(): return lax.ppermute(value, axis, pairs)]
    all_gather x12 -> x0, blocking collectives: 65 us -> none  [carried_in(): everything = lax.all_gather(value, axis)]
    ppermute x24 -> x0, waiting for transfers between devices: 24.6 us -> none  [the longest x12 16.1 us: from_behind(): return lax.ppermute(value, axis, pairs)]
    reduce_sum x10 -> x0, other arithmetic: 11.6 us -> none  [the longest x2 2.95 us: per_device(): move_cap = jnp.sum((cap_mean - cap_first) ** 2)]
    unnamed x40 -> x0, other arithmetic: 7.87 us -> none
    dot_general x7 -> x0, matrix products: 4.41 us -> none  [the longest x6 4.16 us: per_device(): jnp.einsum('xzy,xtzy->t', tonnage_grid, extrapolated, precision=lax.Preci...]
  transfers between devices with their start and end apart: 24 -> 0, of which waited for: 14 -> 0; matrix products, arithmetic and copies ran while one was open for 4% -> 0% of each run, Pallas kernels for 0% -> 0%
where the time goes in v1:
time: 98.1 us; the launch traced here: 97.8 us
  Pallas kernels  90 us (92%)
  local copies, waits for them, and re-layouts  4.76 us (5%)
  between operations  3.1 us (3%)
    pallas_call x1, Pallas kernels, per_device(): pl.pallas_call(functools.partial(kernel, NS, NPD, T, Z, Y, R), out_shape=...  90 us
    unnamed x8, local copies, waits for them, and re-layouts  4.76 us

profile of v1, /device:TPU:0, one launch (start us, length us, event | category | flops | bytes accessed | tf_op | source)
XLA Modules:
  0.0 97.8 jit_solution(8607032212467092530)
XLA Ops:
  1.3 90.0 %shard_map.137 = (f32[1,4,64,128]{3,2,1,0:T(8,128)}, f32[5,1,4,64,128]{4,3,2,1,0:T(8,128)}, f32[1,4,64,128]{3,2,1,0:T(8,128)}, f32[4]{0:T(128)}, f32[1]{0:T(128)}) custom-call(f32[1,4,64,128]{3,2,1,0:T(8,128)} %u_ref.1, f32[5,1,4,64,128]{4,3,2,1,0:T(8,128)} %prec_ref.1, f32[1,4,64,128]{3,2,1,0:T(8,128)} %bound_ref.1, f32[4]{0:T(128)} %cap_ref.1, ...), custom_call_target="tpu_custom_call" | custom-call | tf_op jit(solution)/shard_map/pallas_call | solution.py:371
  91.3 1.6 %copy.21 = f32[1,4,64,128]{3,2,1,0:T(8,128)} copy(f32[1,4,64,128]{3,2,1,0:T(8,128)} %get-tuple-element.10) | data formatting | bytes 262144
  92.8 0.0 copy-start
  92.8 2.0 %copy.22 = f32[5,1,4,64,128]{4,3,2,1,0:T(8,128)} copy(f32[5,1,4,64,128]{4,3,2,1,0:T(8,128)} %get-tuple-element.11) | data formatting | bytes 1310720
  94.9 0.0 copy-done
  94.9 0.0 copy-start.1
  94.9 0.7 copy.23
  95.5 0.0 copy-done.1
  95.5 0.5 copy.24
Async XLA Ops:
  92.8 2.0 %copy-start = (f32[1,4,64,128]{3,2,1,0:T(8,128)S(1)}, f32[1,4,64,128]{3,2,1,0:T(8,128)}, u32[]{:S(2)}) copy-start(f32[1,4,64,128]{3,2,1,0:T(8,128)} %get-tuple-element.12) | copy-start | bytes 393220
  94.9 0.7 copy-start.1

commit v2 on v1

--- a/solution.py
+++ b/solution.py
@@ -23,7 +23,7 @@
     u_out, prec_out, bound_out, cap_out, w_out,
     uf, uc, us, bf, bc, bs, fa, ca, sa, act, ton, tb, tl, cb, ex0,
     xs, xr, es, er, as_, ar, rs, rb, ps, pb, slr,
-    ini_s, ini_r, xs_s, xs_r, e_s, e_r, a_s, a_r, r_s, r_r, p_s, p_r,
+    praw, ti, to_sum, loc, ini_s, ini_r, xs_s, xs_r, e_s, e_r, a_s, a_r, r_s, r_r, p_s, p_r,
 ):
     me = lax.axis_index("strip")
     pe = lax.axis_index("period")
@@ -33,12 +33,18 @@
     root_blocks = math.sqrt(blocks_all)
     sends = []
 
+    loads = (
+        pltpu.make_async_copy(prec_ref.at[:, 0], praw, loc.at[0]),
+        pltpu.make_async_copy(bound_ref.at[0], bf, loc.at[1]),
+        pltpu.make_async_copy(u_ref.at[0], uf, loc.at[2]),
+    )
+    for load in loads:
+        load.start()
     barrier = pltpu.get_barrier_semaphore()
     for k in range(1, NS):
         pl.semaphore_signal(barrier, inc=1, device_id={"strip": lax.rem(me + k, NS)}, device_id_type=MESH)
     for k in range(1, NPD):
         pl.semaphore_signal(barrier, inc=1, device_id={"period": lax.rem(pe + k, NPD)}, device_id_type=MESH)
-    pl.semaphore_wait(barrier, NS + NPD - 2)
 
     has = (me < NS - 1, me > 0)
     gets = (me > 0, me < NS - 1)
@@ -50,8 +56,11 @@
         )
 
     def ini_copy(d, what):
+        if what == 2:
+            return remote(to_sum.at[d], ti.at[d], ini_s.at[d, 2], ini_r.at[d, 2], {"strip": to[d]})
         if what == 0:
-            return remote(prec_ref.at[1 + d, 0], fa.at[5 + d], ini_s.at[d, 0], ini_r.at[d, 0], {"strip": to[d]})
+            rest = pl.ds(1, T - 1)
+            return remote(praw.at[1 + d, rest], fa.at[5 + d, rest], ini_s.at[d, 0], ini_r.at[d, 0], {"strip": to[d]})
         return remote(slope_ref, slr.at[d], ini_s.at[d, 1], ini_r.at[d, 1], {"strip": to[d]})
 
     def x_copy(d, part, s):
@@ -108,9 +117,28 @@
             total = total + rb[slot, k]
         return total
 
+    loads[0].wait()
+    for d in range(2):
+        total = praw[1 + d, 0]
+        for t in range(1, T):
+            total = total + praw[1 + d, t]
+        to_sum[d] = total
+    pl.semaphore_wait(barrier, NS + NPD - 2)
     for d in range(2):
         start(has[d], ini_copy(d, 1))
+        start(has[d], ini_copy(d, 2))
+    for d in range(2):
         start(has[d], ini_copy(d, 0))
+
+    rows = lax.broadcasted_iota(jnp.int32, (R, Y), 0)
+    lanes = lax.broadcasted_iota(jnp.int32, (R, Y), 1)
+
+    def as_lanes(value):
+        sums = jnp.sum(value, axis=1, keepdims=True)
+        return jnp.sum(jnp.where(lanes == rows, sums, 0.0), axis=0, keepdims=True)
+
+    def as_rows(line):
+        return jnp.sum(jnp.where(lanes == rows, line, 0.0), axis=1, keepdims=True)
 
     def fold(v):
         return jnp.sum(v.reshape(Z // 8, 8, Y), axis=0)
@@ -120,9 +148,8 @@
     for c in range(dens_ref.shape[0]):
         tons = jnp.where(cls == c, (1.0 + c) * dens_ref[c], tons)
     ton[...] = tons
-    rows = lax.broadcasted_iota(jnp.int32, (R, Y), 0)
     part = jnp.sum(tons, axis=0, keepdims=True)
-    reduce_start(0, jnp.where(rows == 0, part, 0.0))
+    reduce_start(0, part)
 
     z_ids = lax.broadcasted_iota(jnp.int32, (Z, Y), 0)
     y_ids = lax.broadcasted_iota(jnp.int32, (Z, Y), 1)
@@ -150,12 +177,12 @@
     pid = [jnp.full((1, Y), period[t]) for t in range(T)]
     disc = [jnp.exp(-RATE * pid[t]) for t in range(T)]
     tonr = ton[...] * (1.0 / root_blocks)
+    for load in loads[1:]:
+        load.wait()
     for t in range(T):
         tb[t] = 1.0 / (SLOPE * (total_periods - pid[t]) + tonr)
-        uf[t] = u_ref[0, t]
-        bf[t] = bound_ref[0, t]
         for k in range(5):
-            fa[k, t] = prec_ref[k, 0, t] * act[k]
+            fa[k, t] = praw[k, t] * act[k]
 
     caps = jnp.zeros((R, Y), jnp.float32)
     climit = jnp.zeros((R, Y), jnp.float32)
@@ -168,18 +195,10 @@
         @pl.when(jnp.logical_not(gets[d]))
         def _():
             act[5 + d] = jnp.zeros((Z, Y), jnp.float32)
+            ti[d] = jnp.zeros((Z, Y), jnp.float32)
             fa[5 + d] = jnp.zeros((T, Z, Y), jnp.float32)
             for s in range(STEPS):
                 xr[d, s] = jnp.zeros((T, Z, Y), jnp.float32)
-
-        wait_recv(gets[d], ini_copy(d, 1))
-        wait_recv(gets[d], ini_copy(d, 0))
-
-        @pl.when(gets[d])
-        def _():
-            act[5 + d] = mask_of(slr[d], 1 + d, None)
-            for t in range(T):
-                fa[5 + d, t] = fa[5 + d, t] * act[5 + d]
 
     def up_y(v):
         return pltpu.roll(v, 1, 1)
@@ -219,8 +238,37 @@
         for k in range(1, NPD):
             start(pe >= k, a_copy(k, s))
 
-    gradient(0, fa, bf)
-    tons_all = jnp.sum(jnp.sum(reduce_done(0), axis=0, keepdims=True), axis=1, keepdims=True)
+    tail = None
+    for t in range(T - 1, -1, -1):
+        p = [fa[k, t] for k in range(5)]
+        g = (((p[0] + p[1]) + (p[2] + p[3])) + p[4]) + bf[t]
+        g = g - dn_z(p[0] + (up_y(p[3]) + dn_y(p[4])))
+        tail = g if tail is None else tail + g
+        tl[t] = tail
+    for d in range(2):
+        wait_recv(gets[d], ini_copy(d, 1))
+        wait_recv(gets[d], ini_copy(d, 2))
+
+        @pl.when(gets[d])
+        def _():
+            act[5 + d] = mask_of(slr[d], 1 + d, None)
+    as_[0] = tl[0] - dn_z(ti[0] * act[5] + ti[1] * act[6])
+    for k in range(1, NPD):
+        start(pe >= k, a_copy(k, 0))
+    for d in range(2):
+        wait_recv(gets[d], ini_copy(d, 0))
+        rest = ti[d]
+        for t in range(1, T):
+            plane = fa[5 + d, t]
+            rest = rest - plane
+            fa[5 + d, t] = plane * act[5 + d]
+        fa[5 + d, 0] = rest * act[5 + d]
+    tail = None
+    for t in range(T - 1, -1, -1):
+        back = fa[5, t] + fa[6, t]
+        tail = back if tail is None else tail + back
+        tl[t] = tl[t] - dn_z(tail)
+    tons_all = jnp.sum(reduce_done(0), axis=1, keepdims=True)
     inv_tons = 1.0 / tons_all
     cap_first = cap_sum = None
 
@@ -259,7 +307,7 @@
             start(pe + k < NPD, e_copy(k, s))
         for d in range(2):
             start(has[d], x_copy(d, 0, s))
-        reduce_start(1 + s, row)
+        reduce_start(1 + s, as_lanes(row))
         for k in range(1, NPD):
             @pl.when(pe >= k)
             def _():
@@ -314,8 +362,8 @@
             cyc = s // INNER
             mp = jnp.sum(move_p, axis=0, keepdims=True)
             md = jnp.sum(move_d, axis=0, keepdims=True)
-            reduce_start(1 + STEPS + cyc, jnp.where(rows == 0, mp, jnp.where(rows == 1, md, 0.0)))
-        row_total = jnp.sum(reduce_done(1 + s), axis=1, keepdims=True)
+            reduce_start(1 + STEPS + cyc, as_lanes(jnp.where(rows == 0, mp, jnp.where(rows == 1, md, 0.0))))
+        row_total = as_rows(reduce_done(1 + s))
         new_caps = jnp.maximum(caps + w * ((row_total - climit) * inv_tons), 0.0)
         new_caps = jnp.where(rows < T, new_caps, 0.0)
         if j == 0:
@@ -327,8 +375,8 @@
         if last:
             caps = cap_sum * (1.0 / INNER)
             cap_move = jnp.sum((caps - cap_first) ** 2, axis=0, keepdims=True)
-            got = jnp.sum(reduce_done(1 + STEPS + cyc), axis=1, keepdims=True)
-            msg = jnp.broadcast_to(got, (R, Y)) + jnp.where(rows == 1, cap_move, 0.0)
+            got = reduce_done(1 + STEPS + cyc)
+            msg = got + jnp.where(lanes[0:1] == 1, cap_move, 0.0)
             ps[cyc] = msg
             pb[cyc, pe] = msg
             for k in range(1, NPD):
@@ -345,7 +393,9 @@
             tot = pb[cyc, 0]
             for k in range(1, NPD):
                 tot = tot + pb[cyc, k]
-            w = jnp.sqrt(w * jnp.sqrt((tot[1:2, :] + EPS) / (tot[0:1, :] + EPS)))
+            tot = as_rows(tot)
+            moved = jnp.sqrt((tot[1:2, :] + EPS) / (tot[0:1, :] + EPS))
+            w = jnp.sqrt(w * moved)
     w_out[0] = w[0, 0]
     for cond, copy in sends:
         if cond is None:
@@ -363,6 +413,7 @@
         R = -(-T // 8) * 8
         f32 = jnp.float32
         vmem = pl.BlockSpec(memory_space=pltpu.VMEM)
+        hbm = pl.BlockSpec(memory_space=pl.ANY)
         smem = pl.BlockSpec(memory_space=pltpu.SMEM)
         plane = lambda *n: pltpu.VMEM((*n, Z, Y), f32)
         dma = pltpu.SemaphoreType.DMA
@@ -377,17 +428,18 @@
                 jax.ShapeDtypeStruct(cap.shape, f32),
                 jax.ShapeDtypeStruct((1,), f32),
             ),
-            in_specs=[vmem, vmem, vmem, smem, smem, vmem, vmem, smem, vmem, smem],
+            in_specs=[hbm, hbm, hbm, smem, smem, vmem, vmem, smem, vmem, smem],
             out_specs=(vmem, vmem, vmem, smem, smem),
             scratch_shapes=[
                 plane(T), plane(T), plane(T), plane(T), plane(T), plane(T),
                 plane(7, T), plane(7, T), plane(7, T), plane(7), plane(), plane(T), plane(T), plane(T), plane(),
                 plane(STEPS, T), plane(2, STEPS, T), plane(STEPS), plane(STEPS, far),
                 plane(STEPS), plane(STEPS, far),
-                pltpu.VMEM((slots, R, Y), f32), pltpu.VMEM((slots, NS, R, Y), f32),
-                pltpu.VMEM((OUTER, R, Y), f32), pltpu.VMEM((OUTER, NPD, R, Y), f32),
+                pltpu.VMEM((slots, 1, Y), f32), pltpu.VMEM((slots, NS, 1, Y), f32),
+                pltpu.VMEM((OUTER, 1, Y), f32), pltpu.VMEM((OUTER, NPD, 1, Y), f32),
                 pltpu.VMEM((2, 1, Y), jnp.int32),
-                dma((2, 2)), dma((2, 2)), dma((2, 2, STEPS)), dma((2, 2, STEPS)),
+                plane(5, T), plane(2), plane(2), dma((3,)),
+                dma((2, 3)), dma((2, 3)), dma((2, 2, STEPS)), dma((2, 2, STEPS)),
                 dma((STEPS, far)), dma((STEPS, far)), dma((STEPS, far)), dma((STEPS, far)),
                 dma((slots, NS - 1)), dma((slots, NS - 1)), dma((OUTER, far)), dma((OUTER, far)),
             ],

time: 98.1 us -> 94.8 us (0.966)
  Pallas kernels: 90 us -> 86.6 us
    pallas_call x1, Pallas kernels: 90 us -> 86.6 us  [per_device(): pl.pallas_call(functools.partial(kernel, NS, NPD, T, Z, Y, R), out_shape=...]
where the time goes in v2:
time: 94.8 us; the launch traced here: 94.5 us
  Pallas kernels  86.6 us (91%)
  local copies, waits for them, and re-layouts  4.76 us (5%)
  between operations  3.1 us (3%)
    pallas_call x1, Pallas kernels, per_device(): pl.pallas_call(functools.partial(kernel, NS, NPD, T, Z, Y, R), out_shape=...  86.6 us
    unnamed x8, local copies, waits for them, and re-layouts  4.76 us

profile of v2, /device:TPU:0, one launch (start us, length us, event | category | flops | bytes accessed | tf_op | source)
XLA Modules:
  0.0 94.5 jit_solution(13335256700786077002)
XLA Ops:
  1.3 86.6 %shard_map.137 = (f32[1,4,64,128]{3,2,1,0:T(8,128)}, f32[5,1,4,64,128]{4,3,2,1,0:T(8,128)}, f32[1,4,64,128]{3,2,1,0:T(8,128)}, f32[4]{0:T(128)}, f32[1]{0:T(128)}) custom-call(f32[1,4,64,128]{3,2,1,0:T(8,128)} %u_ref.1, f32[5,1,4,64,128]{4,3,2,1,0:T(8,128)} %prec_ref.1, f32[1,4,64,128]{3,2,1,0:T(8,128)} %bound_ref.1, f32[4]{0:T(128)} %cap_ref.1, ...), custom_call_target="tpu_custom_call" | custom-call | tf_op jit(solution)/shard_map/pallas_call | solution.py:422
  87.9 1.6 %copy.21 = f32[1,4,64,128]{3,2,1,0:T(8,128)} copy(f32[1,4,64,128]{3,2,1,0:T(8,128)} %get-tuple-element.10) | data formatting | bytes 262144
  89.5 0.0 copy-start
  89.5 2.0 %copy.22 = f32[5,1,4,64,128]{4,3,2,1,0:T(8,128)} copy(f32[5,1,4,64,128]{4,3,2,1,0:T(8,128)} %get-tuple-element.11) | data formatting | bytes 1310720
  91.5 0.0 copy-done
  91.5 0.0 copy-start.1
  91.5 0.7 copy.23
  92.2 0.0 copy-done.1
  92.2 0.5 copy.24
Async XLA Ops:
  89.5 2.0 %copy-start = (f32[1,4,64,128]{3,2,1,0:T(8,128)S(1)}, f32[1,4,64,128]{3,2,1,0:T(8,128)}, u32[]{:S(2)}) copy-start(f32[1,4,64,128]{3,2,1,0:T(8,128)} %get-tuple-element.12) | copy-start | bytes 393220
  91.5 0.7 copy-start.1

commit v3 on v2

--- a/solution.py
+++ b/solution.py
@@ -225,13 +225,16 @@
         first[at] = mean
         return mean, fold(diff * diff)
 
-    def gradient(s, arcs, bounds):
+    def gradient_own(arcs, bounds):
+        for t in range(T):
+            p0, p3, p4 = arcs[0, t], arcs[3, t], arcs[4, t]
+            back = p0 + (up_y(p3) + dn_y(p4))
+            tl[t] = ((p0 + p3) + (p4 + bounds[t])) - dn_z(back)
+
+    def gradient(s, arcs):
         tail = None
         for t in range(T - 1, -1, -1):
-            p = [arcs[k, t] for k in range(5)]
-            g = (((p[0] + p[1]) + (p[2] + p[3])) + p[4]) + bounds[t]
-            back = ((p[0] + arcs[5, t]) + arcs[6, t]) + (up_y(p[3]) + dn_y(p[4]))
-            g = g - dn_z(back)
+            g = (tl[t] + (arcs[1, t] + arcs[2, t])) - dn_z(arcs[5, t] + arcs[6, t])
             tail = g if tail is None else tail + g
             tl[t] = tail
         as_[s] = tail
@@ -307,7 +310,6 @@
             start(pe + k < NPD, e_copy(k, s))
         for d in range(2):
             start(has[d], x_copy(d, 0, s))
-        reduce_start(1 + s, as_lanes(row))
         for k in range(1, NPD):
             @pl.when(pe >= k)
             def _():
@@ -316,6 +318,7 @@
         xs[s, 0] = ex0[...]
         for d in range(2):
             start(has[d], x_copy(d, 1, s))
+        reduce_start(1 + s, as_lanes(row))
         total = None
         for t in range(T):
             total = xs[s, t] if t == 0 else total + xs[s, t]
@@ -342,6 +345,9 @@
             move_d = arc(0, t, c - cz, move_d)
             move_d = arc(3, t, c - dn_y(cz), move_d)
             move_d = arc(4, t, c - up_y(cz), move_d)
+        last = j == INNER - 1
+        if s < STEPS - 1:
+            gradient_own(fa if last else ca, bf if last else bc)
         for part in range(2):
             for d in range(2):
                 wait_recv(gets[d], x_copy(d, part, s))
@@ -353,11 +359,11 @@
             cz = up_z(c)
             move_d = arc(1, t, c - up_z(total_p), move_d)
             move_d = arc(2, t, c - up_z(total_m), move_d)
-            move_d = arc(5, t, total_m - cz, move_d)
-            move_d = arc(6, t, total_p - cz, move_d)
-        last = j == INNER - 1
+            if s < STEPS - 1:
+                arc(5, t, total_m - cz, None)
+                arc(6, t, total_p - cz, None)
         if s < STEPS - 1:
-            gradient(s + 1, fa if last else ca, bf if last else bc)
+            gradient(s + 1, fa if last else ca)
         if last:
             cyc = s // INNER
             mp = jnp.sum(move_p, axis=0, keepdims=True)
@@ -422,9 +428,9 @@
         return pl.pallas_call(
             functools.partial(kernel, NS, NPD, T, Z, Y, R),
             out_shape=(
-                jax.ShapeDtypeStruct(u.shape, f32),
-                jax.ShapeDtypeStruct(prec.shape, f32),
-                jax.ShapeDtypeStruct(bound.shape, f32),
+                pltpu.VMEM(u.shape, f32),
+                pltpu.VMEM(prec.shape, f32),
+                pltpu.VMEM(bound.shape, f32),
                 jax.ShapeDtypeStruct(cap.shape, f32),
                 jax.ShapeDtypeStruct((1,), f32),
             ),

time: 94.8 us -> 91.9 us (0.969)
  local copies, waits for them, and re-layouts: 4.76 us -> 2.66 us
    unnamed x8 -> x6, local copies, waits for them, and re-layouts: 4.76 us -> 2.66 us
where the time goes in v3:
time: 91.9 us; the launch traced here: 91.7 us
  Pallas kernels  86 us (94%)
  between operations  3.05 us (3%)
  local copies, waits for them, and re-layouts  2.66 us (3%)
    pallas_call x1, Pallas kernels, per_device(): pl.pallas_call(functools.partial(kernel, NS, NPD, T, Z, Y, R), out_shape=...  86 us
    unnamed x6, local copies, waits for them, and re-layouts  2.66 us

profile of v3, /device:TPU:0, one launch (start us, length us, event | category | flops | bytes accessed | tf_op | source)
XLA Modules:
  0.0 91.7 jit_solution(4046019571566960362)
XLA Ops:
  1.3 86.0 %shard_map.137 = (f32[1,4,64,128]{3,2,1,0:T(8,128)S(1)}, f32[5,1,4,64,128]{4,3,2,1,0:T(8,128)S(1)}, f32[1,4,64,128]{3,2,1,0:T(8,128)S(1)}, f32[4]{0:T(128)}, f32[1]{0:T(128)}) custom-call(f32[1,4,64,128]{3,2,1,0:T(8,128)} %u_ref.1, f32[5,1,4,64,128]{4,3,2,1,0:T(8,128)} %prec_ref.1, f32[1,4,64,128]{3,2,1,0:T(8,128)} %bound_ref.1, f32[4]{0:T(128)} %cap_ref.1, ...), custom_call_target="tpu_custom_call" | custom-call | tf_op jit(solution)/shard_map/pallas_call | solution.py:428
  87.3 0.7 copy.20
  87.9 0.7 copy.22
  88.6 0.0 copy-start
  88.6 0.8 copy.21
  89.4 0.0 copy-done
  89.4 0.5 copy.24
Async XLA Ops:
  88.6 0.8 copy-start
